TPU v7x, 512 devices: a whole 4x8x8 slice. The times are simulated.
512 devices in a mesh: img: 8 (over y_lo, core), cin: 8 (over x, y_hi), cout: 8 (over z).
Axes of the slice: x: 4, y: 8 (y_hi: 2, y_lo: 4; y = y_hi * 4 + y_lo), z: 8, core: 2. Of those that a mesh axis runs over, the one named last changes fastest.
Arguments:
- maps: bfloat16 [2, 8, 14, 14, 1024], P(None, 'img'), may hold values from -6 to 6
- w_first: bfloat16 [3, 3, 1024, 1024], P(None, None, 'cin', 'cout'), may hold values from -0.09375 to 0.09375
- w_reduce: bfloat16 [3, 3, 1024, 8192], P(None, None, 'img', ('cin', 'cout')), may hold values from -0.09375 to 0.09375
- w_wide: bfloat16 [3, 3, 8192, 8192], P(None, None, 'cin', ('img', 'cout')), may hold values from -0.03125 to 0.03125
Outputs:
- wide_out: bfloat16 [2, 8, 7, 7, 8192], P(None, 'cin', None, None, ('img', 'cout'))
All inputs are finite; a program needn't handle non-finite values.
Results may differ from a plain program's by a relative error of at most 0.014.
Values may be sent and summed in bfloat16 or wider, within the bound.
No kernel may reach another device: no remote copies, remote signals or barrier semaphores. Data moves between devices by JAX's collectives and lax.ppermute only.
A program may use at most 64 MiB of HBM per device.

v0:
```python
import jax
import jax.numpy as jnp
from jax import lax
from jax.sharding import PartitionSpec as P


def conv_block(padded, weight_flat, size, step):
    channels = padded.shape[3]
    windows = []
    for row_tap in range(3):
        for col_tap in range(3):
            windows.append(
                padded[
                    :,
                    row_tap : row_tap + step * (size - 1) + 1 : step,
                    col_tap : col_tap + step * (size - 1) + 1 : step,
                    :,
                ]
            )
    table = jnp.concatenate(windows, axis=3).reshape(-1, 9 * channels)
    total = jnp.dot(table, weight_flat, preferred_element_type=jnp.float32)
    return total.reshape(padded.shape[0], size, size, weight_flat.shape[1])


def conv_taps(padded, weight, size, step):
    count = padded.shape[0]
    channels = padded.shape[3]
    weight_flat = weight.reshape(9 * channels, weight.shape[3])
    group = 1
    for trial in range(1, 9):
        if count % trial == 0:
            group = trial
    blocks = padded.reshape(count // group, group, padded.shape[1], padded.shape[2], channels)
    results = lax.map(lambda block: conv_block(block, weight_flat, size, step), blocks)
    return results.reshape(count, size, size, weight.shape[3])


def pad_map(values):
    return jnp.pad(values, ((0, 0), (1, 1), (1, 1), (0, 0)))


def local(maps, w_first, w_reduce, w_wide):
    batches = maps.shape[0]
    side = maps.shape[2]
    half = side // 2
    in_block = w_first.shape[2]
    out_block = w_first.shape[3]
    flat = maps.reshape(-1, side, side, maps.shape[4])
    in_part = lax.dynamic_slice_in_dim(flat, lax.axis_index("cin") * in_block, in_block, 3)
    first_terms = conv_taps(pad_map(jnp.maximum(in_part, 0)), w_first, side, 1)
    first_terms = first_terms.reshape(batches, maps.shape[1], side, side, out_block)
    summed = lax.psum(first_terms, "cin")
    own_part = lax.dynamic_slice_in_dim(maps, lax.axis_index("cout") * out_block, out_block, 4)
    segment_maps = (own_part.astype(jnp.float32) + summed).astype(jnp.bfloat16)
    whole = lax.all_gather(segment_maps, "cout", axis=4, tiled=True)
    by_channel = lax.all_to_all(whole, "img", split_axis=4, concat_axis=1, tiled=True)
    images = by_channel.shape[1]
    rect_segment = jnp.maximum(by_channel, 0).reshape(-1, side, side, by_channel.shape[4])
    reduced = conv_taps(pad_map(rect_segment), w_reduce, half, 2).reshape(
        batches, images, half, half, w_reduce.shape[3]
    )
    out_width = w_wide.shape[3]
    summed_wide = lax.psum(reduced, "img")
    narrow = jnp.maximum(summed_wide, 0.0).astype(jnp.bfloat16)
    gathered = lax.all_gather(narrow, "cout", axis=4, tiled=True)
    flat_all = gathered.reshape(-1, half, half, gathered.shape[4])
    partial_value = conv_taps(pad_map(flat_all), w_wide, half, 1)
    partial_value = partial_value.reshape(batches, images, half, half, out_width)
    result = lax.psum_scatter(
        partial_value.astype(jnp.bfloat16), "cin", scatter_dimension=1, tiled=True
    )
    return result


def solution(mesh):
    in_specs = (
        P(None, "img", None, None, None),
        P(None, None, "cin", "cout"),
        P(None, None, "img", ("cin", "cout")),
        P(None, None, "cin", ("img", "cout")),
    )
    out_specs = P(None, "cin", None, None, ("img", "cout"))
    return jax.shard_map(local, mesh=mesh, in_specs=in_specs, out_specs=out_specs, check_vma=False)
```

profile of v0, /device:TPU:64, one launch (start us, length us, event | category | flops | bytes accessed | tf_op | source)
XLA Modules:
  0.0 461.7 jit_solution(14591765025077755233)
XLA Ops:
  6.5 1.1 constant_dynamic-slice_fusion.2
  7.8 0.1 slice_dynamic-update-slice_fusion.23
  7.8 0.1 slice_dynamic-update-slice_fusion.22
  8.0 0.1 slice_dynamic-update-slice_fusion.21
  8.0 0.1 slice_dynamic-update-slice_fusion.20
  8.1 0.1 slice_dynamic-update-slice_fusion.18
  8.2 1.1 convolution_bitcast_fusion.1
  9.3 116.6 %all-reduce.8.cloned.1.call-done = f32[2,1,14,14,128]{4,3,2,0,1:T(8,128)} async-done(((f32[2,1,14,14,128]{4,3,2,0,1:T(8,128)}), f32[2,1,14,14,128]{4,3,2,0,1:T(8,128)}) %all-reduce.8.cloned.1.call-update) | async-done | bytes 200720 | tf_op jit(solution)/shard_map/psum | solution.py:52
  126.0 1.0 add_convert_fusion
  126.9 26.5 %all_gather.6 = bf16[2,1,14,14,1024]{4,3,2,0,1:T(8,128)(2,1)S(1)} all-gather(bf16[2,1,14,14,128]{4,3,2,0,1:T(8,128)(2,1)S(1)} %add_convert_fusion), channel_id=1, replica_groups=mesh['img'=8,'cin'=8,'cout'=8] {'cout'}, dimensions={4}, use_global_device_ids=true | all-gather | bytes 903168 | tf_op jit(solution)/shard_map/all_gather | solution.py:55
  153.5 12.4 %copy.42 = bf16[2,1,14,14,1024]{3,0,2,1,4:T(2,128)(2,1)} copy(bf16[2,1,14,14,1024]{4,3,2,0,1:T(8,128)(2,1)S(1)} %all_gather.6) | data formatting | bytes 1605632 | tf_op jit(solution)/shard_map/all_gather | solution.py:55
  165.8 12.8 %reshape.68 = bf16[8,2,25088]{2,1,0:T(2,128)(2,1)} reshape(bf16[1024,1,14,2,14]{4,3,2,1,0:T(2,128)(2,1)} %bitcast.84) | data formatting | bytes 1605632
  178.7 3.5 all-to-all-start
  182.3 21.2 %all-to-all-done = bf16[8,2,25088]{2,1,0:T(2,128)(2,1)S(1)} async-done(((bf16[8,2,25088]{2,1,0:T(2,128)(2,1)}), bf16[8,2,25088]{2,1,0:T(2,128)(2,1)S(1)}, u32[]{:S(2)}, u32[]{:S(2)}) %all-to-all-start) | async-done | bytes 802848 | tf_op jit(solution)/shard_map/all_to_all | solution.py:56
  203.4 19.8 %reshape.69 = bf16[1024,1,14,2,14]{4,3,2,1,0:T(2,128)(2,1)} reshape(bf16[8,2,25088]{2,1,0:T(2,128)(2,1)S(1)} %all-to-all-done) | data formatting | bytes 1605632
  223.2 17.3 %copy.43 = bf16[2,1,14,14,1024]{4,0,3,2,1:T(2,128)(2,1)S(1)} copy(bf16[2,1,14,14,1024]{3,0,2,1,4:T(2,128)(2,1)} %bitcast.85) | data formatting | bytes 1605632 | tf_op jit(solution)/shard_map/all_to_all | solution.py:56
  240.5 0.7 broadcast_maximum_fusion
  241.2 0.5 max.33
  241.7 1.2 pad_bitcast_fusion.1
  242.9 4.0 while.26
  242.9 1.2 dynamic-slice_bitcast_fusion.6
  244.5 0.4 fusion.26
  245.0 1.1 dynamic-slice_bitcast_fusion.6
  246.4 0.4 fusion.26
  246.9 31.9 %all-reduce.11 = bf16[2,8,7,7,128]{4,1,0,3,2:T(8,128)(2,1)S(1)} all-reduce(f32[2,8,7,7,128]{4,1,0,3,2:T(8,128)S(1)} %get-tuple-element.61), channel_id=1, replica_groups=mesh['img'=8,'cin'=8,'cout'=8] {'img'}, use_global_device_ids=true, to_apply=%region_3.4 | all-reduce | flops 100352 | bytes 602112 | tf_op jit(solution)/shard_map/psum | solution.py:63
  278.8 0.7 maximum_convert_fusion
  279.6 41.6 %all-gather.2.cloned.1.call-done = bf16[2,8,7,7,1024]{4,1,0,3,2:T(8,128)(2,1)} async-done(((bf16[2,8,7,7,128]{4,1,0,3,2:T(8,128)(2,1)}), bf16[2,8,7,7,1024]{4,1,0,3,2:T(8,128)(2,1)}) %all-gather.2.cloned.1.call-update) | async-done | bytes 1605648 | tf_op jit(solution)/shard_map/all_gather | solution.py:65
  321.2 3.3 pad_bitcast_fusion
  324.5 17.2 %while.27 = (s32[]{:T(128)}, bf16[2,8,7,7,128]{4,0,3,2,1:T(2,128)(2,1)S(1)}, bf16[2,8,9,9,1024]{4,1,0,3,2:T(8,128)(2,1)}, bf16[9216,128]{1,0:T(8,128)(2,1)S(1)}) while((s32[]{:T(128)}, bf16[2,8,7,7,128]{4,0,3,2,1:T(2,128)(2,1)S(1)}, bf16[2,8,9,9,1024]{4,1,0,3,2:T(8,128)(2,1)}, bf16[9216,128]{1,0:T(8,128)(2,1)S(1)}) %tuple.60), condition=%wide.region_5.6_spmd.clone, body=%wide.region_4.5_spmd.sunk.clone | while | flops 924844032 | bytes 27191356 | solution.py:34
  324.5 1.4 dynamic-slice_bitcast_fusion.7
  326.0 0.1 slice_dynamic-update-slice_fusion.72
  326.1 0.1 slice_dynamic-update-slice_fusion.73
  326.3 0.1 slice_dynamic-update-slice_fusion.76
  326.3 0.1 slice_dynamic-update-slice_fusion.77
  326.5 2.0 fusion.29
  328.6 0.2 copy.72
  328.7 4.4 dynamic_update_slice.16
  333.1 1.4 dynamic-slice_bitcast_fusion.7
  334.7 0.1 slice_dynamic-update-slice_fusion.73
  334.8 0.1 slice_dynamic-update-slice_fusion.74
  334.9 0.1 slice_dynamic-update-slice_fusion.77
  335.1 2.0 fusion.29
  337.2 0.2 copy.72
  337.3 4.4 dynamic_update_slice.16
  341.8 0.7 copy-done.3
  342.5 1.3 dynamic-slice.2
  343.7 109.5 %all-reduce.10.cloned.1.call-done = bf16[2,8,7,7,128]{4,0,3,2,1:T(2,128)(2,1)} async-done(((bf16[2,8,7,7,128]{4,0,3,2,1:T(2,128)(2,1)}), bf16[2,8,7,7,128]{4,0,3,2,1:T(2,128)(2,1)}) %all-reduce.10.cloned.1.call-update) | async-done | bytes 200720
  453.3 1.9 constant_dynamic-slice_fusion
  (49 shorter events, 1.6 us)
Async XLA Ops:
  6.5 1.6 copy-start
  6.5 119.4 %all-reduce.8.cloned.1.call-start = ((), (), s32[]{:S(2)}) async-start(), calls=%async_computation.1 | async-start | bytes 458752 | tf_op jit(solution)/shard_map/psum | solution.py:52
  178.7 24.8 %all-to-all-start = ((bf16[8,2,25088]{2,1,0:T(2,128)(2,1)}), bf16[8,2,25088]{2,1,0:T(2,128)(2,1)S(1)}, u32[]{:S(2)}, u32[]{:S(2)}) async-start(bf16[8,2,25088]{2,1,0:T(2,128)(2,1)} %reshape.68), calls=%async_computation | async-start | bytes 1605632 | tf_op jit(solution)/shard_map/all_to_all | solution.py:56
  182.2 139.0 %all-gather.2.cloned.1.call-start = ((), (), s32[]{:S(2)}) async-start(), calls=%async_computation.2 | async-start | bytes 1806336 | tf_op jit(solution)/shard_map/all_gather | solution.py:65
  223.2 19.7 %copy-start.2 = (bf16[3,3,128,128]{3,2,1,0:T(8,128)(2,1)S(1)}, bf16[3,3,128,128]{3,2,1,0:T(8,128)(2,1)}, u32[]{:S(2)}) copy-start(bf16[3,3,128,128]{3,2,1,0:T(8,128)(2,1)} %param.10) | copy-start | bytes 884740
  242.9 81.6 %copy-start.1 = (bf16[3,3,1024,128]{3,2,1,0:T(8,128)(2,1)S(1)}, bf16[3,3,1024,128]{3,2,1,0:T(8,128)(2,1)}, u32[]{:S(2)}) copy-start(bf16[3,3,1024,128]{3,2,1,0:T(8,128)(2,1)} %param.11) | copy-start | bytes 7077892
  279.5 173.7 %all-reduce.10.cloned.1.call-start = ((), (), s32[]{:S(2)}) async-start(), calls=%async_computation.3 | async-start | bytes 401408
  341.8 0.7 copy-start.3
Sparse Core Ops, SparseCore 0:
  10.3 115.6 all-reduce.7
  279.6 41.5 all-gather.1
  342.6 110.6 all-reduce.9
where the time goes:
time: 463 us; the launch traced here: 462 us
  waiting for transfers between devices  289 us (62%)
  local copies, waits for them, and re-layouts  88.5 us (19%)
  blocking collectives  58.4 us (13%)
  between operations  13.3 us (3%)
  matrix products  6.06 us (1%)
    psum x1, waiting for transfers between devices, local(): summed = lax.psum(first_terms, 'cin')  117 us
    unnamed x4, waiting for transfers between devices  110 us
    all_gather x1, waiting for transfers between devices, local(): gathered = lax.all_gather(narrow, 'cout', axis=4, tiled=True)  41.6 us
    unnamed x19, local copies, waits for them, and re-layouts  36.8 us
    psum x1, blocking collectives, local(): summed_wide = lax.psum(reduced, 'img')  31.9 us
    all_gather x1, blocking collectives, local(): whole = lax.all_gather(segment_maps, 'cout', axis=4, tiled=True)  26.5 us
    all_to_all x1, waiting for transfers between devices, local(): lax.all_to_all(whole, 'img', split_axis=4, concat_axis=1, tiled=True)  21.2 us
    all_to_all x1, local copies, waits for them, and re-layouts, local(): lax.all_to_all(whole, 'img', split_axis=4, concat_axis=1, tiled=True)  17.3 us
  transfers between devices with their start and end apart: 4, of which 4 were waited for; matrix products, arithmetic and copies ran while one was open for 0% of the time, Pallas kernels for 0%

commit v1 on v0

--- a/solution.py
+++ b/solution.py
@@ -53,7 +53,10 @@
     own_part = lax.dynamic_slice_in_dim(maps, lax.axis_index("cout") * out_block, out_block, 4)
     segment_maps = (own_part.astype(jnp.float32) + summed).astype(jnp.bfloat16)
     whole = lax.all_gather(segment_maps, "cout", axis=4, tiled=True)
-    by_channel = lax.all_to_all(whole, "img", split_axis=4, concat_axis=1, tiled=True)
+    devices = lax.axis_size("img")
+    pieces = jnp.stack(jnp.split(whole, devices, axis=4), axis=0)
+    pieces = lax.all_to_all(pieces, "img", split_axis=0, concat_axis=0)
+    by_channel = jnp.concatenate(pieces, axis=1)
     images = by_channel.shape[1]
     rect_segment = jnp.maximum(by_channel, 0).reshape(-1, side, side, by_channel.shape[4])
     reduced = conv_taps(pad_map(rect_segment), w_reduce, half, 2).reshape(

time: 463 us -> 401 us (0.87)
  local copies, waits for them, and re-layouts: 88.5 us -> 27.6 us
    unnamed x19 -> x24, local copies, waits for them, and re-layouts: 36.8 us -> 4.5 us
    all_to_all x1 -> x0, local copies, waits for them, and re-layouts: 17.3 us -> none  [local(): lax.all_to_all(whole, 'img', split_axis=4, concat_axis=1, tiled=True)]
    all_gather x1 -> x0, local copies, waits for them, and re-layouts: 12.4 us -> none  [local(): whole = lax.all_gather(segment_maps, 'cout', axis=4, tiled=True)]
where the time goes in v1:
time: 401 us; the launch traced here: 400 us
  waiting for transfers between devices  289 us (72%)
  blocking collectives  58.4 us (15%)
  local copies, waits for them, and re-layouts  27.6 us (7%)
  between operations  13.2 us (3%)
  matrix products  6.06 us (2%)
    psum x1, waiting for transfers between devices, local(): summed = lax.psum(first_terms, 'cin')  117 us
    unnamed x4, waiting for transfers between devices  109 us
    all_gather x1, waiting for transfers between devices, local(): gathered = lax.all_gather(narrow, 'cout', axis=4, tiled=True)  41.6 us
    psum x1, blocking collectives, local(): summed_wide = lax.psum(reduced, 'img')  31.9 us
    all_gather x1, blocking collectives, local(): whole = lax.all_gather(segment_maps, 'cout', axis=4, tiled=True)  26.5 us
    all_to_all x1, waiting for transfers between devices, local(): pieces = lax.all_to_all(pieces, 'img', split_axis=0, concat_axis=0)  21.2 us
    dynamic_update_slice x4, local copies, waits for them, and re-layouts, conv_taps(): lax.map(lambda block: conv_block(block, weight_flat, size, step), blocks)  9.11 us
  transfers between devices with their start and end apart: 4, of which 4 were waited for; matrix products, arithmetic and copies ran while one was open for 0% of the time, Pallas kernels for 0%

profile of v1, /device:TPU:64, one launch (start us, length us, event | category | flops | bytes accessed | tf_op | source)
XLA Modules:
  0.0 400.1 jit_solution(10652155590075912570)
XLA Ops:
  6.5 1.1 constant_dynamic-slice_fusion.2
  7.8 0.1 slice_dynamic-update-slice_fusion.23
  7.9 0.1 slice_dynamic-update-slice_fusion.22
  8.0 0.1 slice_dynamic-update-slice_fusion.21
  8.0 0.1 slice_dynamic-update-slice_fusion.20
  8.1 0.1 slice_dynamic-update-slice_fusion.18
  8.2 1.1 convolution_bitcast_fusion.1
  9.4 116.6 %all-reduce.8.cloned.1.call-done = f32[2,1,14,14,128]{4,3,2,0,1:T(8,128)} async-done(((f32[2,1,14,14,128]{4,3,2,0,1:T(8,128)}), f32[2,1,14,14,128]{4,3,2,0,1:T(8,128)}) %all-reduce.8.cloned.1.call-update) | async-done | bytes 200720 | tf_op jit(solution)/shard_map/psum | solution.py:52
  126.0 1.0 add_convert_fusion
  126.9 26.5 %all_gather.6 = bf16[2,1,14,14,1024]{4,3,2,0,1:T(8,128)(2,1)S(1)} all-gather(bf16[2,1,14,14,128]{4,3,2,0,1:T(8,128)(2,1)S(1)} %add_convert_fusion), channel_id=1, replica_groups=mesh['img'=8,'cin'=8,'cout'=8] {'cout'}, dimensions={4}, use_global_device_ids=true | all-gather | bytes 903168 | tf_op jit(solution)/shard_map/all_gather | solution.py:55
  153.8 1.5 copy.20
  155.3 3.5 all-to-all-start
  158.9 21.2 %all-to-all-done = bf16[8,2,1,14,14,128]{5,1,4,3,2,0:T(2,128)(2,1)S(1)} async-done(((bf16[8,2,1,14,14,128]{5,1,4,3,2,0:T(2,128)(2,1)}), bf16[8,2,1,14,14,128]{5,1,4,3,2,0:T(2,128)(2,1)S(1)}, u32[]{:S(2)}, u32[]{:S(2)}) %all-to-all-start) | async-done | bytes 802848 | tf_op jit(solution)/shard_map/all_to_all | solution.py:58
  180.1 0.1 fusion.7
  180.2 1.2 pad_bitcast_fusion.1
  181.4 4.0 while.26
  181.4 1.2 dynamic-slice_bitcast_fusion.6
  183.0 0.4 fusion.35
  183.5 1.1 dynamic-slice_bitcast_fusion.6
  184.9 0.4 fusion.35
  185.4 31.9 %all-reduce.11 = bf16[2,8,7,7,128]{4,1,0,3,2:T(8,128)(2,1)S(1)} all-reduce(f32[2,8,7,7,128]{4,1,0,3,2:T(8,128)S(1)} %get-tuple-element.61), channel_id=1, replica_groups=mesh['img'=8,'cin'=8,'cout'=8] {'img'}, use_global_device_ids=true, to_apply=%region_3.4 | all-reduce | flops 100352 | bytes 602112 | tf_op jit(solution)/shard_map/psum | solution.py:66
  217.3 0.7 maximum_convert_fusion
  218.1 41.6 %all-gather.2.cloned.1.call-done = bf16[2,8,7,7,1024]{4,1,0,3,2:T(8,128)(2,1)} async-done(((bf16[2,8,7,7,128]{4,1,0,3,2:T(8,128)(2,1)}), bf16[2,8,7,7,1024]{4,1,0,3,2:T(8,128)(2,1)}) %all-gather.2.cloned.1.call-update) | async-done | bytes 1605648 | tf_op jit(solution)/shard_map/all_gather | solution.py:68
  259.7 3.3 pad_bitcast_fusion
  263.0 17.2 %while.27 = (s32[]{:T(128)}, bf16[2,8,7,7,128]{4,0,3,2,1:T(2,128)(2,1)S(1)}, bf16[2,8,9,9,1024]{4,1,0,3,2:T(8,128)(2,1)}, bf16[9216,128]{1,0:T(8,128)(2,1)S(1)}) while((s32[]{:T(128)}, bf16[2,8,7,7,128]{4,0,3,2,1:T(2,128)(2,1)S(1)}, bf16[2,8,9,9,1024]{4,1,0,3,2:T(8,128)(2,1)}, bf16[9216,128]{1,0:T(8,128)(2,1)S(1)}) %tuple.56), condition=%wide.region_5.6_spmd.clone, body=%wide.region_4.5_spmd.sunk.clone | while | flops 924844032 | bytes 27191356 | solution.py:34
  263.0 1.4 dynamic-slice_bitcast_fusion.7
  264.5 0.1 slice_dynamic-update-slice_fusion.72
  264.6 0.1 slice_dynamic-update-slice_fusion.73
  264.6 0.1 slice_dynamic-update-slice_fusion.74
  264.7 0.1 slice_dynamic-update-slice_fusion.75
  264.8 0.1 slice_dynamic-update-slice_fusion.76
  265.0 0.1 slice_dynamic-update-slice_fusion.79
  265.0 2.0 fusion.38
  267.1 0.2 copy.53
  267.2 4.4 %dynamic_update_slice.16 = bf16[2,8,7,7,128]{4,0,3,2,1:T(2,128)(2,1)S(1)} dynamic-update-slice(bf16[2,8,7,7,128]{4,0,3,2,1:T(2,128)(2,1)S(1)} %get-tuple-element.185, bf16[1,8,7,7,128]{4,0,3,2,1:T(2,128)(2,1)S(1)} %copy.53, s32[]{:T(128)} %get-tuple-element.184, s32[]{:T(128)} %constant.29.clone.1..sunk.1, s32[]{:T(128)} %constant.29.clone.1..sunk.1, s32[]{:T(128)} %constant.29.clone.1..sunk.1, ...) | dynamic-update-slice | bytes 200708 | tf_op jit(solution)/shard_map/while/body/jit(dynamic_update_index_in_dim)/dynamic_update_slice | solution.py:34
  271.6 1.4 dynamic-slice_bitcast_fusion.7
  273.1 0.1 slice_dynamic-update-slice_fusion.72
  273.3 0.1 slice_dynamic-update-slice_fusion.75
  273.4 0.1 slice_dynamic-update-slice_fusion.76
  273.5 0.1 slice_dynamic-update-slice_fusion.78
  273.6 0.1 slice_dynamic-update-slice_fusion.79
  273.6 2.0 fusion.38
  275.7 0.2 copy.53
  275.8 4.4 %dynamic_update_slice.16 = bf16[2,8,7,7,128]{4,0,3,2,1:T(2,128)(2,1)S(1)} dynamic-update-slice(bf16[2,8,7,7,128]{4,0,3,2,1:T(2,128)(2,1)S(1)} %get-tuple-element.185, bf16[1,8,7,7,128]{4,0,3,2,1:T(2,128)(2,1)S(1)} %copy.53, s32[]{:T(128)} %get-tuple-element.184, s32[]{:T(128)} %constant.29.clone.1..sunk.1, s32[]{:T(128)} %constant.29.clone.1..sunk.1, s32[]{:T(128)} %constant.29.clone.1..sunk.1, ...) | dynamic-update-slice | bytes 200708 | tf_op jit(solution)/shard_map/while/body/jit(dynamic_update_index_in_dim)/dynamic_update_slice | solution.py:34
  280.3 0.7 copy-done.3
  281.0 1.3 dynamic-slice.2
  282.2 109.4 %all-reduce.10.cloned.1.call-done = bf16[2,8,7,7,128]{4,0,3,2,1:T(2,128)(2,1)} async-done(((bf16[2,8,7,7,128]{4,0,3,2,1:T(2,128)(2,1)}), bf16[2,8,7,7,128]{4,0,3,2,1:T(2,128)(2,1)}) %all-reduce.10.cloned.1.call-update) | async-done | bytes 200720
  391.7 1.9 constant_dynamic-slice_fusion
  (53 shorter events, 1.7 us)
Async XLA Ops:
  6.5 1.7 copy-start
  6.5 119.4 %all-reduce.8.cloned.1.call-start = ((), (), s32[]{:S(2)}) async-start(), calls=%async_computation.1 | async-start | bytes 458752 | tf_op jit(solution)/shard_map/psum | solution.py:52
  6.5 174.9 %copy-start.2 = (bf16[3,3,128,128]{3,2,1,0:T(8,128)(2,1)S(1)}, bf16[3,3,128,128]{3,2,1,0:T(8,128)(2,1)}, u32[]{:S(2)}) copy-start(bf16[3,3,128,128]{3,2,1,0:T(8,128)(2,1)} %param.10) | copy-start | bytes 884740
  155.3 24.8 %all-to-all-start = ((bf16[8,2,1,14,14,128]{5,1,4,3,2,0:T(2,128)(2,1)}), bf16[8,2,1,14,14,128]{5,1,4,3,2,0:T(2,128)(2,1)S(1)}, u32[]{:S(2)}, u32[]{:S(2)}) async-start(bf16[8,2,1,14,14,128]{5,1,4,3,2,0:T(2,128)(2,1)} %copy.20), calls=%async_computation | async-start | bytes 1605632 | tf_op jit(solution)/shard_map/all_to_all | solution.py:58
  158.9 100.9 %all-gather.2.cloned.1.call-start = ((), (), s32[]{:S(2)}) async-start(), calls=%async_computation.2 | async-start | bytes 1806336 | tf_op jit(solution)/shard_map/all_gather | solution.py:68
  181.4 81.6 %copy-start.1 = (bf16[3,3,1024,128]{3,2,1,0:T(8,128)(2,1)S(1)}, bf16[3,3,1024,128]{3,2,1,0:T(8,128)(2,1)}, u32[]{:S(2)}) copy-start(bf16[3,3,1024,128]{3,2,1,0:T(8,128)(2,1)} %param.11) | copy-start | bytes 7077892
  218.0 173.6 %all-reduce.10.cloned.1.call-start = ((), (), s32[]{:S(2)}) async-start(), calls=%async_computation.3 | async-start | bytes 401408
  280.3 0.7 copy-start.3
Sparse Core Ops, SparseCore 0:
  10.3 115.6 all-reduce.7
  218.2 41.5 all-gather.1
  281.1 110.5 all-reduce.9
